TPU v7x, 256 devices: a whole 4x4x8 slice. The times are simulated.
256 devices in a mesh: pb: 32 (over x, y, z_lo), row: 8 (over z_hi, core).
Axes of the slice: x: 4, y: 4, z: 8 (z_hi: 4, z_lo: 2; z = z_hi * 2 + z_lo), core: 2. Of those that a mesh axis runs over, the one named last changes fastest.
Arguments:
- query_desc: bfloat16 [16384, 512], P(('pb', 'row')), may hold values from -6 to 6
- ref_desc: bfloat16 [12288, 512], P(('row', 'pb')), may hold values from -6 to 6
- taps: float32 [2, 8], replicated, may hold values from -1.3 to 1.3
Outputs:
- aligned: float32 [16384, 12288], P('pb', 'row')
All inputs are finite; a program needn't handle non-finite values.
Results may differ from a plain program's by a relative error of at most 0.0003.
Values may be sent and summed in bfloat16 or wider, within the bound.
No kernel may reach another device: no remote copies, remote signals or barrier semaphores. Data moves between devices by JAX's collectives and lax.ppermute only.
A program may use at most 64 MiB of HBM per device.

v0:
```python
import jax
import jax.numpy as jnp
from jax import lax
from jax.sharding import PartitionSpec as P

DESC = 512
DILATION_STEP = 32
TAP_COUNT = 8


def padded(value, sides, width):
    for axis, dim in sides:
        count, length = (lax.axis_size(axis), value.shape[dim])
        up = [(i, (i + 1) % count) for i in range(count - 1)]
        down = [(j, i) for i, j in up]
        last = lax.slice_in_dim(value, length - width, length, axis=dim)
        leading = lax.slice_in_dim(value, 0, width, axis=dim)
        before = lax.ppermute(last, axis, up)
        after = lax.ppermute(leading, axis, down)
        value = jnp.concatenate([before, value, after], axis=dim)
    return value


def diagonal_pass(padded_matrix, tap_weights, output_rows, output_columns):
    total_reach = jnp.zeros((output_rows, output_columns), jnp.float32)
    for tap_index in range(TAP_COUNT):
        total_reach = (
            total_reach
            + tap_weights[tap_index]
            * padded_matrix[
                tap_index * DILATION_STEP : tap_index * DILATION_STEP + output_rows,
                tap_index * DILATION_STEP : tap_index * DILATION_STEP + output_columns,
            ]
        )
    return jnp.tanh(total_reach)


def inner_scores(left, right):
    return lax.dot_general(
        left, right, (((1,), (1,)), ((), ())), preferred_element_type=jnp.float32
    )


def pass_rims(receptive_field):
    return padded(receptive_field, (("pb", 0), ("row", 1)), TAP_COUNT * DILATION_STEP // 2)


def local(query_desc, ref_desc, taps):
    scale = DESC ** (-0.5)
    queries = lax.all_gather(query_desc, "row", axis=0, tiled=True)
    rows = queries.shape[0]
    cols = ref_desc.shape[0] * lax.axis_size("pb")
    sim = inner_scores(queries, lax.all_gather(ref_desc, "pb", axis=0, tiled=True))
    base = jnp.tanh(sim * scale)
    first = diagonal_pass(pass_rims(base), taps[0], rows, cols)
    return diagonal_pass(pass_rims(first), taps[1], rows, cols)


def solution(mesh):
    in_specs = (P(("pb", "row"), None), P(("row", "pb"), None), P())
    out_specs = P("pb", "row")
    return jax.shard_map(local, mesh=mesh, in_specs=in_specs, out_specs=out_specs, check_vma=False)
```

profile of v0, /device:TPU:23, one launch (start us, length us, event | category | flops | bytes accessed | tf_op | source)
XLA Modules:
  0.0 300.0 jit_solution(13734901324448696239)
XLA Ops:
  7.3 19.4 %all_gather.6 = bf16[512,512]{1,0:T(8,128)(2,1)S(1)} all-gather(bf16[64,512]{1,0:T(8,128)(2,1)} %param.3), channel_id=1, replica_groups=mesh['pb'=32,'row'=8] {'row'}, dimensions={0}, use_global_device_ids=true | all-gather | bytes 589824 | tf_op jit(solution)/shard_map/all_gather | solution.py:50
  26.6 113.1 %all-gather.2.cloned.1.call-done = bf16[1536,512]{1,0:T(8,128)(2,1)} async-done(((bf16[48,512]{1,0:T(8,128)(2,1)}), bf16[1536,512]{1,0:T(8,128)(2,1)}) %all-gather.2.cloned.1.call-update) | async-done | bytes 1572880 | tf_op jit(solution)/shard_map/all_gather | solution.py:53
  139.8 2.4 fusion
  142.3 6.7 %collective-permute-start = (f32[128,1536]{1,0:T(8,128)S(1)}, f32[128,1536]{1,0:T(8,128)S(1)}, u32[]{:S(2)}, u32[]{:S(2)}) collective-permute-start(f32[128,1536]{1,0:T(8,128)S(1)} %get-tuple-element.15), channel_id=1, source_target_pairs={{0,8},{8,16},{16,24},{24,32},{32,40},{40,48},{48,56},{56,64},{64,7... | collective-permute-start | bytes 2359304 | tf_op jit(solution)/shard_map/ppermute | solution.py:18
  149.0 1.9 collective-permute-start.1
  151.0 8.0 %collective-permute-done = f32[128,1536]{1,0:T(8,128)S(1)} collective-permute-done((f32[128,1536]{1,0:T(8,128)S(1)}, f32[128,1536]{1,0:T(8,128)S(1)}, u32[]{:S(2)}, u32[]{:S(2)}) %collective-permute-start) | collective-permute-done | bytes 786464 | tf_op jit(solution)/shard_map/ppermute | solution.py:18
  158.9 9.3 %collective-permute-done.1 = f32[128,1536]{1,0:T(8,128)S(1)} collective-permute-done((f32[128,1536]{1,0:T(8,128)S(1)}, f32[128,1536]{1,0:T(8,128)S(1)}, u32[]{:S(2)}, u32[]{:S(2)}) %collective-permute-start.1) | collective-permute-done | bytes 786464 | tf_op jit(solution)/shard_map/ppermute | solution.py:19
  168.3 25.3 %collective-permute-start.2 = (f32[768,128]{1,0:T(8,128)S(1)}, f32[768,128]{1,0:T(8,128)S(1)}, u32[]{:S(2)}, u32[]{:S(2)}) collective-permute-start(f32[768,128]{1,0:T(8,128)S(1)} %get-tuple-element.11), channel_id=1, source_target_pairs={{0,1},{1,2},{2,3},{3,4},{4,5},{5,6},{6,7},{8,9},{9,10},{10,11},{11... | collective-permute-start | bytes 1179656 | tf_op jit(solution)/shard_map/ppermute | solution.py:18
  193.7 1.9 collective-permute-start.3
  195.6 0.7 fusion.19
  196.3 2.0 collective-permute-done.2
  198.4 5.3 %collective-permute-done.3 = f32[768,128]{1,0:T(8,128)S(1)} collective-permute-done((f32[768,128]{1,0:T(8,128)S(1)}, f32[768,128]{1,0:T(8,128)S(1)}, u32[]{:S(2)}, u32[]{:S(2)}) %collective-permute-start.3) | collective-permute-done | bytes 393248 | tf_op jit(solution)/shard_map/ppermute | solution.py:19
  203.7 3.2 %maximum_maximum_fusion = (f32[768,1664]{1,0:T(8,128)S(1)}, f32[768,1664]{1,0:T(8,128)S(1)}) fusion(f32[128,1536]{1,0:T(8,128)S(1)} %collective-permute-done.1, f32[512,1536]{1,0:T(8,128)S(1)} %fusion, f32[128,1536]{1,0:T(8,128)S(1)} %collective-permute-done, f32[768,128]{1,0:T(8,128)S(1)} %collective-permute-done.2, f32[768,128]{1,0:T(8,128)S(1)} %collective-permute-done.3), kind=kLoop, calls=%fused_computation | loop fusion | flops 7667712 | bytes 15728640 | tf_op jit(solution)/shard_map/concatenate | solution.py:20
  206.8 10.2 %fusion.10 = f32[512,1536]{1,0:T(8,128)S(1)} fusion(f32[768,1664]{1,0:T(8,128)S(1)} %get-tuple-element.10, f32[768,1664]{1,0:T(8,128)S(1)} %get-tuple-element.9, f32[512,1536]{1,0:T(8,128)S(1)} %fusion, f32[]{:T(128)} %bitcast.8, f32[]{:T(128)} %bitcast.7, f32[]{:T(128)} %bitcast.6, f32[]{:T(128)} %bitcast.5, f32[]{:T(128)} %bitcast.4, f32[]{:T(128)} %bitcast.3, ...), kind=kLoop, calls=%fused_computation.23 | loop fusion | flops 11796480 | bytes 28311584 | tf_op jit(solution)/shard_map/tanh | solution.py:35
  217.1 11.6 %collective-permute-start.4 = (f32[128,1536]{1,0:T(8,128)S(1)}, f32[128,1536]{1,0:T(8,128)S(1)}, u32[]{:S(2)}, u32[]{:S(2)}) collective-permute-start(f32[128,1536]{1,0:T(8,128)S(1)} %get-tuple-element.13), channel_id=1, source_target_pairs={{0,8},{8,16},{16,24},{24,32},{32,40},{40,48},{48,56},{56,64},{64,7... | collective-permute-start | bytes 2359304 | tf_op jit(solution)/shard_map/ppermute | solution.py:18
  228.7 1.9 collective-permute-start.5
  230.6 15.4 %collective-permute-done.4 = f32[128,1536]{1,0:T(8,128)S(1)} collective-permute-done((f32[128,1536]{1,0:T(8,128)S(1)}, f32[128,1536]{1,0:T(8,128)S(1)}, u32[]{:S(2)}, u32[]{:S(2)}) %collective-permute-start.4) | collective-permute-done | bytes 786464 | tf_op jit(solution)/shard_map/ppermute | solution.py:18
  246.0 11.1 %collective-permute-done.5 = f32[128,1536]{1,0:T(8,128)S(1)} collective-permute-done((f32[128,1536]{1,0:T(8,128)S(1)}, f32[128,1536]{1,0:T(8,128)S(1)}, u32[]{:S(2)}, u32[]{:S(2)}) %collective-permute-start.5) | collective-permute-done | bytes 786464 | tf_op jit(solution)/shard_map/ppermute | solution.py:19
  257.2 8.3 %collective-permute-start.6 = (f32[768,128]{1,0:T(8,128)S(1)}, f32[768,128]{1,0:T(8,128)S(1)}, u32[]{:S(2)}, u32[]{:S(2)}) collective-permute-start(f32[768,128]{1,0:T(8,128)S(1)} %get-tuple-element.7), channel_id=1, source_target_pairs={{0,1},{1,2},{2,3},{3,4},{4,5},{5,6},{6,7},{8,9},{9,10},{10,11},{11... | collective-permute-start | bytes 1179656 | tf_op jit(solution)/shard_map/ppermute | solution.py:18
  265.5 1.9 collective-permute-start.7
  267.4 2.8 collective-permute-done.6
  270.2 8.5 %collective-permute-done.7 = f32[768,128]{1,0:T(8,128)S(1)} collective-permute-done((f32[768,128]{1,0:T(8,128)S(1)}, f32[768,128]{1,0:T(8,128)S(1)}, u32[]{:S(2)}, u32[]{:S(2)}) %collective-permute-start.7) | collective-permute-done | bytes 393248 | tf_op jit(solution)/shard_map/ppermute | solution.py:19
  278.8 3.2 %maximum_maximum_fusion.1 = (f32[768,1664]{1,0:T(8,128)S(1)}, f32[768,1664]{1,0:T(8,128)S(1)}) fusion(f32[128,1536]{1,0:T(8,128)S(1)} %collective-permute-done.5, f32[512,1536]{1,0:T(8,128)S(1)} %fusion.10, f32[128,1536]{1,0:T(8,128)S(1)} %collective-permute-done.4, f32[768,128]{1,0:T(8,128)S(1)} %collective-permute-done.6, ...), kind=kLoop, calls=%fused_computation.2 | loop fusion | flops 7667712 | bytes 15728640 | tf_op jit(solution)/shard_map/concatenate | solution.py:20
  281.9 11.2 %fusion.2 = f32[512,1536]{1,0:T(8,128)} fusion(f32[768,1664]{1,0:T(8,128)S(1)} %get-tuple-element.6, f32[768,1664]{1,0:T(8,128)S(1)} %get-tuple-element.5, f32[512,1536]{1,0:T(8,128)S(1)} %fusion.10, f32[]{:T(128)} %bitcast.15, f32[]{:T(128)} %bitcast.14, f32[]{:T(128)} %bitcast.13, f32[]{:T(128)} %bitcast.12, f32[]{:T(128)} %bitcast.11, f32[]{:T(128)} %bitcast.10, ...), kind=kLoop, calls=%fused_computation.8 | loop fusion | flops 11796480 | bytes 28311584 | tf_op jit(solution)/shard_map/tanh | solution.py:35
  (8 shorter events, 1.0 us)
Async XLA Ops:
  6.5 133.2 %all-gather.2.cloned.1.call-start = ((), (), s32[]{:S(2)}) async-start(), calls=%async_computation | async-start | bytes 1622016 | tf_op jit(solution)/shard_map/all_gather | solution.py:53
  142.3 53.3 %copy-start = (f32[2,8]{1,0:T(2,128)S(1)}, f32[2,8]{1,0:T(2,128)}, u32[]{:S(2)}) copy-start(f32[2,8]{1,0:T(2,128)} %param.5) | copy-start | bytes 196
  142.3 16.6 %collective-permute-start = (f32[128,1536]{1,0:T(8,128)S(1)}, f32[128,1536]{1,0:T(8,128)S(1)}, u32[]{:S(2)}, u32[]{:S(2)}) collective-permute-start(f32[128,1536]{1,0:T(8,128)S(1)} %get-tuple-element.15), channel_id=1, source_target_pairs={{0,8},{8,16},{16,24},{24,32},{32,40},{40,48},{48,56},{56,64},{64,7... | collective-permute-start | bytes 2359304 | tf_op jit(solution)/shard_map/ppermute | solution.py:18
  149.0 19.2 %collective-permute-start.1 = (f32[128,1536]{1,0:T(8,128)S(1)}, f32[128,1536]{1,0:T(8,128)S(1)}, u32[]{:S(2)}, u32[]{:S(2)}) collective-permute-start(f32[128,1536]{1,0:T(8,128)S(1)} %get-tuple-element.16), channel_id=1, source_target_pairs={{8,0},{16,8},{24,16},{32,24},{40,32},{48,40},{56,48},{64,56},{72,6... | collective-permute-start | bytes 2359304 | tf_op jit(solution)/shard_map/ppermute | solution.py:19
  168.3 30.0 %collective-permute-start.2 = (f32[768,128]{1,0:T(8,128)S(1)}, f32[768,128]{1,0:T(8,128)S(1)}, u32[]{:S(2)}, u32[]{:S(2)}) collective-permute-start(f32[768,128]{1,0:T(8,128)S(1)} %get-tuple-element.11), channel_id=1, source_target_pairs={{0,1},{1,2},{2,3},{3,4},{4,5},{5,6},{6,7},{8,9},{9,10},{10,11},{11... | collective-permute-start | bytes 1179656 | tf_op jit(solution)/shard_map/ppermute | solution.py:18
  193.7 10.0 %collective-permute-start.3 = (f32[768,128]{1,0:T(8,128)S(1)}, f32[768,128]{1,0:T(8,128)S(1)}, u32[]{:S(2)}, u32[]{:S(2)}) collective-permute-start(f32[768,128]{1,0:T(8,128)S(1)} %get-tuple-element.12), channel_id=1, source_target_pairs={{1,0},{2,1},{3,2},{4,3},{5,4},{6,5},{7,6},{9,8},{10,9},{11,10},{12... | collective-permute-start | bytes 1179656 | tf_op jit(solution)/shard_map/ppermute | solution.py:19
  217.1 28.9 %collective-permute-start.4 = (f32[128,1536]{1,0:T(8,128)S(1)}, f32[128,1536]{1,0:T(8,128)S(1)}, u32[]{:S(2)}, u32[]{:S(2)}) collective-permute-start(f32[128,1536]{1,0:T(8,128)S(1)} %get-tuple-element.13), channel_id=1, source_target_pairs={{0,8},{8,16},{16,24},{24,32},{32,40},{40,48},{48,56},{56,64},{64,7... | collective-permute-start | bytes 2359304 | tf_op jit(solution)/shard_map/ppermute | solution.py:18
  228.7 28.5 %collective-permute-start.5 = (f32[128,1536]{1,0:T(8,128)S(1)}, f32[128,1536]{1,0:T(8,128)S(1)}, u32[]{:S(2)}, u32[]{:S(2)}) collective-permute-start(f32[128,1536]{1,0:T(8,128)S(1)} %get-tuple-element.14), channel_id=1, source_target_pairs={{8,0},{16,8},{24,16},{32,24},{40,32},{48,40},{56,48},{64,56},{72,6... | collective-permute-start | bytes 2359304 | tf_op jit(solution)/shard_map/ppermute | solution.py:19
  257.2 13.0 %collective-permute-start.6 = (f32[768,128]{1,0:T(8,128)S(1)}, f32[768,128]{1,0:T(8,128)S(1)}, u32[]{:S(2)}, u32[]{:S(2)}) collective-permute-start(f32[768,128]{1,0:T(8,128)S(1)} %get-tuple-element.7), channel_id=1, source_target_pairs={{0,1},{1,2},{2,3},{3,4},{4,5},{5,6},{6,7},{8,9},{9,10},{10,11},{11... | collective-permute-start | bytes 1179656 | tf_op jit(solution)/shard_map/ppermute | solution.py:18
  265.5 13.3 %collective-permute-start.7 = (f32[768,128]{1,0:T(8,128)S(1)}, f32[768,128]{1,0:T(8,128)S(1)}, u32[]{:S(2)}, u32[]{:S(2)}) collective-permute-start(f32[768,128]{1,0:T(8,128)S(1)} %get-tuple-element.8), channel_id=1, source_target_pairs={{1,0},{2,1},{3,2},{4,3},{5,4},{6,5},{7,6},{9,8},{10,9},{11,10},{12... | collective-permute-start | bytes 1179656 | tf_op jit(solution)/shard_map/ppermute | solution.py:19
Sparse Core Ops, SparseCore 0:
  9.1 130.5 all-gather.1
where the time goes:
time: 300 us
  waiting for transfers between devices  176 us (59%)
  starting transfers between devices  59.6 us (20%)
  other arithmetic  27.8 us (9%)
  blocking collectives  19.4 us (6%)
  between operations  13.5 us (4%)
    all_gather x1, waiting for transfers between devices, local(): lax.all_gather(ref_desc, 'pb', axis=0, tiled=True)  113 us
    ppermute x4, starting transfers between devices, padded(): before = lax.ppermute(last, axis, up)  51.9 us
    ppermute x4, waiting for transfers between devices, padded(): after = lax.ppermute(leading, axis, down)  34.3 us
    ppermute x4, waiting for transfers between devices, padded(): before = lax.ppermute(last, axis, up)  28.2 us
    tanh x2, other arithmetic, diagonal_pass(): return jnp.tanh(total_reach)  21.4 us
    all_gather x1, blocking collectives, local(): queries = lax.all_gather(query_desc, 'row', axis=0, tiled=True)  19.4 us
    ppermute x4, starting transfers between devices, padded(): after = lax.ppermute(leading, axis, down)  7.68 us
    concatenate x2, other arithmetic, padded(): value = jnp.concatenate([before, value, after], axis=dim)  6.3 us
  transfers between devices with their start and end apart: 9, of which 9 were waited for; matrix products, arithmetic and copies ran while one was open for 0% of the time, Pallas kernels for 0%

commit v1 on v0

--- a/solution.py
+++ b/solution.py
@@ -6,6 +6,13 @@
 DESC = 512
 DILATION_STEP = 32
 TAP_COUNT = 8
+
+
+def answer_stages_all(in_array):
+    samples = []
+    for _ in range(jax.lax.axis_size("pb")):
+        samples.append(in_array)
+    return jnp.concatenate(jax.lax.all_to_all(jnp.stack(samples, axis=0), "pb", 0, 0), 0)
 
 
 def padded(value, sides, width):
@@ -50,7 +57,7 @@
     queries = lax.all_gather(query_desc, "row", axis=0, tiled=True)
     rows = queries.shape[0]
     cols = ref_desc.shape[0] * lax.axis_size("pb")
-    sim = inner_scores(queries, lax.all_gather(ref_desc, "pb", axis=0, tiled=True))
+    sim = inner_scores(queries, answer_stages_all(ref_desc))
     base = jnp.tanh(sim * scale)
     first = diagonal_pass(pass_rims(base), taps[0], rows, cols)
     return diagonal_pass(pass_rims(first), taps[1], rows, cols)

time: 300 us -> 186 us (0.62)
  waiting for transfers between devices: 176 us -> 75.4 us
  starting transfers between devices: 59.6 us -> 43.9 us
  blocking collectives: 19.4 us -> 33.3 us
  between operations: 13.5 us -> 0.16 us
    all_gather x1 -> x0, waiting for transfers between devices: 113 us -> none  [local(): lax.all_gather(ref_desc, 'pb', axis=0, tiled=True)]
    ppermute x4, starting transfers between devices: 51.9 us -> 27.6 us  [padded(): before = lax.ppermute(last, axis, up)]
    all_gather x1, blocking collectives: 19.4 us -> 33.3 us  [local(): queries = lax.all_gather(query_desc, 'row', axis=0, tiled=True)]
    all_to_all x0 -> x1, starting transfers between devices: none -> 8.2 us  [answer_stages_all(): jax.lax.all_to_all(jnp.stack(samples, axis=0), 'pb', 0, 0)]
    ppermute x4, waiting for transfers between devices: 28.2 us -> 35.8 us  [padded(): before = lax.ppermute(last, axis, up)]
    ppermute x4, waiting for transfers between devices: 34.3 us -> 39.7 us  [padded(): after = lax.ppermute(leading, axis, down)]
  transfers between devices with their start and end apart: 9 -> 9, of which waited for: 9 -> 8; matrix products, arithmetic and copies ran while one was open for 0% -> 0% of each run, Pallas kernels for 0% -> 0%
where the time goes in v1:
time: 186 us; the launch traced here: 185 us
  waiting for transfers between devices  75.4 us (41%)
  starting transfers between devices  43.9 us (24%)
  blocking collectives  33.3 us (18%)
  other arithmetic  27.8 us (15%)
  local copies, waits for them, and re-layouts  3.09 us (2%)
    ppermute x4, waiting for transfers between devices, padded(): after = lax.ppermute(leading, axis, down)  39.7 us
    ppermute x4, waiting for transfers between devices, padded(): before = lax.ppermute(last, axis, up)  35.8 us
    all_gather x1, blocking collectives, local(): queries = lax.all_gather(query_desc, 'row', axis=0, tiled=True)  33.3 us
    ppermute x4, starting transfers between devices, padded(): before = lax.ppermute(last, axis, up)  27.6 us
    tanh x2, other arithmetic, diagonal_pass(): return jnp.tanh(total_reach)  21.4 us
    all_to_all x1, starting transfers between devices, answer_stages_all(): jax.lax.all_to_all(jnp.stack(samples, axis=0), 'pb', 0, 0)  8.2 us
    ppermute x4, starting transfers between devices, padded(): after = lax.ppermute(leading, axis, down)  8.11 us
    concatenate x2, other arithmetic, padded(): value = jnp.concatenate([before, value, after], axis=dim)  6.3 us
  transfers between devices with their start and end apart: 9, of which 8 were waited for; matrix products, arithmetic and copies ran while one was open for 0% of the time, Pallas kernels for 0%

profile of v1, /device:TPU:23, one launch (start us, length us, event | category | flops | bytes accessed | tf_op | source)
XLA Modules:
  0.0 184.8 jit_solution(12857873339579453230)
XLA Ops:
  0.0 2.1 %stack.2 = bf16[32,48,512]{2,1,0:T(8,128)(2,1)} broadcast(bf16[48,512]{1,0:T(8,128)(2,1)} %param.4), dimensions={1,2} | broadcast | bytes 1622016 | tf_op jit(solution)/shard_map/stack | solution.py:15
  2.2 8.2 %all-to-all-start = ((bf16[32,48,512]{2,1,0:T(8,128)(2,1)}), bf16[32,48,512]{2,1,0:T(8,128)(2,1)S(1)}, u32[]{:S(2)}, u32[]{:S(2)}) async-start(bf16[32,48,512]{2,1,0:T(8,128)(2,1)} %stack.2), calls=%async_computation | async-start | bytes 3145728 | tf_op jit(solution)/shard_map/all_to_all | solution.py:15
  10.4 33.3 %all_gather.3 = bf16[512,512]{1,0:T(8,128)(2,1)S(1)} all-gather(bf16[64,512]{1,0:T(8,128)(2,1)S(1)} %copy-done), channel_id=1, replica_groups=mesh['pb'=32,'row'=8] {'row'}, dimensions={0}, use_global_device_ids=true | all-gather | bytes 589824 | tf_op jit(solution)/shard_map/all_gather | solution.py:57
  43.7 1.0 fusion
  44.8 3.8 %collective-permute-start = (f32[128,1536]{1,0:T(8,128)S(1)}, f32[128,1536]{1,0:T(8,128)S(1)}, u32[]{:S(2)}, u32[]{:S(2)}) collective-permute-start(f32[128,1536]{1,0:T(8,128)S(1)} %get-tuple-element.15), channel_id=1, source_target_pairs={{0,8},{8,16},{16,24},{24,32},{32,40},{40,48},{48,56},{56,64},{64,7... | collective-permute-start | bytes 2359304 | tf_op jit(solution)/shard_map/ppermute | solution.py:25
  48.7 2.3 %collective-permute-start.1 = (f32[128,1536]{1,0:T(8,128)S(1)}, f32[128,1536]{1,0:T(8,128)S(1)}, u32[]{:S(2)}, u32[]{:S(2)}) collective-permute-start(f32[128,1536]{1,0:T(8,128)S(1)} %get-tuple-element.16), channel_id=1, source_target_pairs={{8,0},{16,8},{24,16},{32,24},{40,32},{48,40},{56,48},{64,56},{72,6... | collective-permute-start | bytes 2359304 | tf_op jit(solution)/shard_map/ppermute | solution.py:26
  51.0 15.5 %collective-permute-done = f32[128,1536]{1,0:T(8,128)S(1)} collective-permute-done((f32[128,1536]{1,0:T(8,128)S(1)}, f32[128,1536]{1,0:T(8,128)S(1)}, u32[]{:S(2)}, u32[]{:S(2)}) %collective-permute-start) | collective-permute-done | bytes 786464 | tf_op jit(solution)/shard_map/ppermute | solution.py:25
  66.5 16.5 %collective-permute-done.1 = f32[128,1536]{1,0:T(8,128)S(1)} collective-permute-done((f32[128,1536]{1,0:T(8,128)S(1)}, f32[128,1536]{1,0:T(8,128)S(1)}, u32[]{:S(2)}, u32[]{:S(2)}) %collective-permute-start.1) | collective-permute-done | bytes 786464 | tf_op jit(solution)/shard_map/ppermute | solution.py:26
  83.1 5.5 %collective-permute-start.2 = (f32[768,128]{1,0:T(8,128)S(1)}, f32[768,128]{1,0:T(8,128)S(1)}, u32[]{:S(2)}, u32[]{:S(2)}) collective-permute-start(f32[768,128]{1,0:T(8,128)S(1)} %get-tuple-element.11), channel_id=1, source_target_pairs={{0,1},{1,2},{2,3},{3,4},{4,5},{5,6},{6,7},{8,9},{9,10},{10,11},{11... | collective-permute-start | bytes 1179656 | tf_op jit(solution)/shard_map/ppermute | solution.py:25
  88.6 1.9 %collective-permute-start.3 = (f32[768,128]{1,0:T(8,128)S(1)}, f32[768,128]{1,0:T(8,128)S(1)}, u32[]{:S(2)}, u32[]{:S(2)}) collective-permute-start(f32[768,128]{1,0:T(8,128)S(1)} %get-tuple-element.12), channel_id=1, source_target_pairs={{1,0},{2,1},{3,2},{4,3},{5,4},{6,5},{7,6},{9,8},{10,9},{11,10},{12... | collective-permute-start | bytes 1179656 | tf_op jit(solution)/shard_map/ppermute | solution.py:26
  91.3 2.0 %collective-permute-done.2 = f32[768,128]{1,0:T(8,128)S(1)} collective-permute-done((f32[768,128]{1,0:T(8,128)S(1)}, f32[768,128]{1,0:T(8,128)S(1)}, u32[]{:S(2)}, u32[]{:S(2)}) %collective-permute-start.2) | collective-permute-done | bytes 393248 | tf_op jit(solution)/shard_map/ppermute | solution.py:25
  93.3 5.3 %collective-permute-done.3 = f32[768,128]{1,0:T(8,128)S(1)} collective-permute-done((f32[768,128]{1,0:T(8,128)S(1)}, f32[768,128]{1,0:T(8,128)S(1)}, u32[]{:S(2)}, u32[]{:S(2)}) %collective-permute-start.3) | collective-permute-done | bytes 393248 | tf_op jit(solution)/shard_map/ppermute | solution.py:26
  98.6 3.2 %maximum_maximum_fusion = (f32[768,1664]{1,0:T(8,128)S(1)}, f32[768,1664]{1,0:T(8,128)S(1)}) fusion(f32[128,1536]{1,0:T(8,128)S(1)} %collective-permute-done.1, f32[512,1536]{1,0:T(8,128)S(1)} %fusion, f32[128,1536]{1,0:T(8,128)S(1)} %collective-permute-done, f32[768,128]{1,0:T(8,128)S(1)} %collective-permute-done.2, f32[768,128]{1,0:T(8,128)S(1)} %collective-permute-done.3), kind=kLoop, calls=%fused_computation | loop fusion | flops 7667712 | bytes 15728640 | tf_op jit(solution)/shard_map/concatenate | solution.py:27
  101.8 10.2 %fusion.10 = f32[512,1536]{1,0:T(8,128)S(1)} fusion(f32[768,1664]{1,0:T(8,128)S(1)} %get-tuple-element.10, f32[768,1664]{1,0:T(8,128)S(1)} %get-tuple-element.9, f32[512,1536]{1,0:T(8,128)S(1)} %fusion, f32[]{:T(128)} %bitcast.9, f32[]{:T(128)} %bitcast.8, f32[]{:T(128)} %bitcast.7, f32[]{:T(128)} %bitcast.6, f32[]{:T(128)} %bitcast.5, f32[]{:T(128)} %bitcast.4, ...), kind=kLoop, calls=%fused_computation.23 | loop fusion | flops 11796480 | bytes 28311584 | tf_op jit(solution)/shard_map/tanh | solution.py:42
  112.1 8.1 %collective-permute-start.4 = (f32[128,1536]{1,0:T(8,128)S(1)}, f32[128,1536]{1,0:T(8,128)S(1)}, u32[]{:S(2)}, u32[]{:S(2)}) collective-permute-start(f32[128,1536]{1,0:T(8,128)S(1)} %get-tuple-element.13), channel_id=1, source_target_pairs={{0,8},{8,16},{16,24},{24,32},{32,40},{40,48},{48,56},{56,64},{64,7... | collective-permute-start | bytes 2359304 | tf_op jit(solution)/shard_map/ppermute | solution.py:25
  120.2 1.9 %collective-permute-start.5 = (f32[128,1536]{1,0:T(8,128)S(1)}, f32[128,1536]{1,0:T(8,128)S(1)}, u32[]{:S(2)}, u32[]{:S(2)}) collective-permute-start(f32[128,1536]{1,0:T(8,128)S(1)} %get-tuple-element.14), channel_id=1, source_target_pairs={{8,0},{16,8},{24,16},{32,24},{40,32},{48,40},{56,48},{64,56},{72,6... | collective-permute-start | bytes 2359304 | tf_op jit(solution)/shard_map/ppermute | solution.py:26
  122.1 15.4 %collective-permute-done.4 = f32[128,1536]{1,0:T(8,128)S(1)} collective-permute-done((f32[128,1536]{1,0:T(8,128)S(1)}, f32[128,1536]{1,0:T(8,128)S(1)}, u32[]{:S(2)}, u32[]{:S(2)}) %collective-permute-start.4) | collective-permute-done | bytes 786464 | tf_op jit(solution)/shard_map/ppermute | solution.py:25
  137.5 9.1 %collective-permute-done.5 = f32[128,1536]{1,0:T(8,128)S(1)} collective-permute-done((f32[128,1536]{1,0:T(8,128)S(1)}, f32[128,1536]{1,0:T(8,128)S(1)}, u32[]{:S(2)}, u32[]{:S(2)}) %collective-permute-start.5) | collective-permute-done | bytes 786464 | tf_op jit(solution)/shard_map/ppermute | solution.py:26
  146.7 10.2 %collective-permute-start.6 = (f32[768,128]{1,0:T(8,128)S(1)}, f32[768,128]{1,0:T(8,128)S(1)}, u32[]{:S(2)}, u32[]{:S(2)}) collective-permute-start(f32[768,128]{1,0:T(8,128)S(1)} %get-tuple-element.7), channel_id=1, source_target_pairs={{0,1},{1,2},{2,3},{3,4},{4,5},{5,6},{6,7},{8,9},{9,10},{10,11},{11... | collective-permute-start | bytes 1179656 | tf_op jit(solution)/shard_map/ppermute | solution.py:25
  156.9 1.9 %collective-permute-start.7 = (f32[768,128]{1,0:T(8,128)S(1)}, f32[768,128]{1,0:T(8,128)S(1)}, u32[]{:S(2)}, u32[]{:S(2)}) collective-permute-start(f32[768,128]{1,0:T(8,128)S(1)} %get-tuple-element.8), channel_id=1, source_target_pairs={{1,0},{2,1},{3,2},{4,3},{5,4},{6,5},{7,6},{9,8},{10,9},{11,10},{12... | collective-permute-start | bytes 1179656 | tf_op jit(solution)/shard_map/ppermute | solution.py:26
  158.8 2.8 %collective-permute-done.6 = f32[768,128]{1,0:T(8,128)S(1)} collective-permute-done((f32[768,128]{1,0:T(8,128)S(1)}, f32[768,128]{1,0:T(8,128)S(1)}, u32[]{:S(2)}, u32[]{:S(2)}) %collective-permute-start.6) | collective-permute-done | bytes 393248 | tf_op jit(solution)/shard_map/ppermute | solution.py:25
  161.6 8.7 %collective-permute-done.7 = f32[768,128]{1,0:T(8,128)S(1)} collective-permute-done((f32[768,128]{1,0:T(8,128)S(1)}, f32[768,128]{1,0:T(8,128)S(1)}, u32[]{:S(2)}, u32[]{:S(2)}) %collective-permute-start.7) | collective-permute-done | bytes 393248 | tf_op jit(solution)/shard_map/ppermute | solution.py:26
  170.3 3.2 %maximum_maximum_fusion.1 = (f32[768,1664]{1,0:T(8,128)S(1)}, f32[768,1664]{1,0:T(8,128)S(1)}) fusion(f32[128,1536]{1,0:T(8,128)S(1)} %collective-permute-done.5, f32[512,1536]{1,0:T(8,128)S(1)} %fusion.10, f32[128,1536]{1,0:T(8,128)S(1)} %collective-permute-done.4, f32[768,128]{1,0:T(8,128)S(1)} %collective-permute-done.6, ...), kind=kLoop, calls=%fused_computation.2 | loop fusion | flops 7667712 | bytes 15728640 | tf_op jit(solution)/shard_map/concatenate | solution.py:27
  173.5 11.2 %fusion.2 = f32[512,1536]{1,0:T(8,128)} fusion(f32[768,1664]{1,0:T(8,128)S(1)} %get-tuple-element.6, f32[768,1664]{1,0:T(8,128)S(1)} %get-tuple-element.5, f32[512,1536]{1,0:T(8,128)S(1)} %fusion.10, f32[]{:T(128)} %bitcast.16, f32[]{:T(128)} %bitcast.15, f32[]{:T(128)} %bitcast.14, f32[]{:T(128)} %bitcast.13, f32[]{:T(128)} %bitcast.12, f32[]{:T(128)} %bitcast.11, ...), kind=kLoop, calls=%fused_computation.8 | loop fusion | flops 11796480 | bytes 28311584 | tf_op jit(solution)/shard_map/tanh | solution.py:42
  (10 shorter events, 1.0 us)
Async XLA Ops:
  0.0 10.4 %copy-start = (bf16[64,512]{1,0:T(8,128)(2,1)S(1)}, bf16[64,512]{1,0:T(8,128)(2,1)}, u32[]{:S(2)}) copy-start(bf16[64,512]{1,0:T(8,128)(2,1)} %param.3) | copy-start | bytes 196612
  2.2 41.5 %all-to-all-start = ((bf16[32,48,512]{2,1,0:T(8,128)(2,1)}), bf16[32,48,512]{2,1,0:T(8,128)(2,1)S(1)}, u32[]{:S(2)}, u32[]{:S(2)}) async-start(bf16[32,48,512]{2,1,0:T(8,128)(2,1)} %stack.2), calls=%async_computation | async-start | bytes 3145728 | tf_op jit(solution)/shard_map/all_to_all | solution.py:15
  44.8 45.8 %copy-start.1 = (f32[2,8]{1,0:T(2,128)S(1)}, f32[2,8]{1,0:T(2,128)}, u32[]{:S(2)}) copy-start(f32[2,8]{1,0:T(2,128)} %param.5) | copy-start | bytes 196
  44.8 21.7 %collective-permute-start = (f32[128,1536]{1,0:T(8,128)S(1)}, f32[128,1536]{1,0:T(8,128)S(1)}, u32[]{:S(2)}, u32[]{:S(2)}) collective-permute-start(f32[128,1536]{1,0:T(8,128)S(1)} %get-tuple-element.15), channel_id=1, source_target_pairs={{0,8},{8,16},{16,24},{24,32},{32,40},{40,48},{48,56},{56,64},{64,7... | collective-permute-start | bytes 2359304 | tf_op jit(solution)/shard_map/ppermute | solution.py:25
  48.7 34.4 %collective-permute-start.1 = (f32[128,1536]{1,0:T(8,128)S(1)}, f32[128,1536]{1,0:T(8,128)S(1)}, u32[]{:S(2)}, u32[]{:S(2)}) collective-permute-start(f32[128,1536]{1,0:T(8,128)S(1)} %get-tuple-element.16), channel_id=1, source_target_pairs={{8,0},{16,8},{24,16},{32,24},{40,32},{48,40},{56,48},{64,56},{72,6... | collective-permute-start | bytes 2359304 | tf_op jit(solution)/shard_map/ppermute | solution.py:26
  83.1 10.2 %collective-permute-start.2 = (f32[768,128]{1,0:T(8,128)S(1)}, f32[768,128]{1,0:T(8,128)S(1)}, u32[]{:S(2)}, u32[]{:S(2)}) collective-permute-start(f32[768,128]{1,0:T(8,128)S(1)} %get-tuple-element.11), channel_id=1, source_target_pairs={{0,1},{1,2},{2,3},{3,4},{4,5},{5,6},{6,7},{8,9},{9,10},{10,11},{11... | collective-permute-start | bytes 1179656 | tf_op jit(solution)/shard_map/ppermute | solution.py:25
  88.6 10.0 %collective-permute-start.3 = (f32[768,128]{1,0:T(8,128)S(1)}, f32[768,128]{1,0:T(8,128)S(1)}, u32[]{:S(2)}, u32[]{:S(2)}) collective-permute-start(f32[768,128]{1,0:T(8,128)S(1)} %get-tuple-element.12), channel_id=1, source_target_pairs={{1,0},{2,1},{3,2},{4,3},{5,4},{6,5},{7,6},{9,8},{10,9},{11,10},{12... | collective-permute-start | bytes 1179656 | tf_op jit(solution)/shard_map/ppermute | solution.py:26
  112.1 25.4 %collective-permute-start.4 = (f32[128,1536]{1,0:T(8,128)S(1)}, f32[128,1536]{1,0:T(8,128)S(1)}, u32[]{:S(2)}, u32[]{:S(2)}) collective-permute-start(f32[128,1536]{1,0:T(8,128)S(1)} %get-tuple-element.13), channel_id=1, source_target_pairs={{0,8},{8,16},{16,24},{24,32},{32,40},{40,48},{48,56},{56,64},{64,7... | collective-permute-start | bytes 2359304 | tf_op jit(solution)/shard_map/ppermute | solution.py:25
  120.2 26.5 %collective-permute-start.5 = (f32[128,1536]{1,0:T(8,128)S(1)}, f32[128,1536]{1,0:T(8,128)S(1)}, u32[]{:S(2)}, u32[]{:S(2)}) collective-permute-start(f32[128,1536]{1,0:T(8,128)S(1)} %get-tuple-element.14), channel_id=1, source_target_pairs={{8,0},{16,8},{24,16},{32,24},{40,32},{48,40},{56,48},{64,56},{72,6... | collective-permute-start | bytes 2359304 | tf_op jit(solution)/shard_map/ppermute | solution.py:26
  146.7 14.9 %collective-permute-start.6 = (f32[768,128]{1,0:T(8,128)S(1)}, f32[768,128]{1,0:T(8,128)S(1)}, u32[]{:S(2)}, u32[]{:S(2)}) collective-permute-start(f32[768,128]{1,0:T(8,128)S(1)} %get-tuple-element.7), channel_id=1, source_target_pairs={{0,1},{1,2},{2,3},{3,4},{4,5},{5,6},{6,7},{8,9},{9,10},{10,11},{11... | collective-permute-start | bytes 1179656 | tf_op jit(solution)/shard_map/ppermute | solution.py:25
  156.9 13.5 %collective-permute-start.7 = (f32[768,128]{1,0:T(8,128)S(1)}, f32[768,128]{1,0:T(8,128)S(1)}, u32[]{:S(2)}, u32[]{:S(2)}) collective-permute-start(f32[768,128]{1,0:T(8,128)S(1)} %get-tuple-element.8), channel_id=1, source_target_pairs={{1,0},{2,1},{3,2},{4,3},{5,4},{6,5},{7,6},{9,8},{10,9},{11,10},{12... | collective-permute-start | bytes 1179656 | tf_op jit(solution)/shard_map/ppermute | solution.py:26
